TPU v7x, 32 devices: a whole 2x2x4 slice. The times are simulated.
32 devices in a mesh: blk: 4 (over y, x), team: 4 (over z), dp: 2 (over core).
Axes of the slice: x: 2, y: 2, z: 4, core: 2. Of those that a mesh axis runs over, the one named last changes fastest.
Arguments:
- hidden: bfloat16 [1024, 28672], P(('blk', 'dp'), 'team'), may hold values from -6 to 6
- out_grad: bfloat16 [1024, 8192], P(('blk', 'dp'), 'team'), may hold values from -0.1875 to 0.1875
- act_rows: int32 [4, 64, 12], P('team'), may hold values from 0 to 55, as said below
- col_owner: int32 [64], replicated, may hold values from 0 to 3, as said below
Outputs:
- gradients: float32 [4, 4, 288, 128, 128], P('team', 'blk', 'dp')
- scores: float32 [4, 4, 288], P('team', 'blk', 'dp')
Inputs may be any that keep to these rules, and one draw needn't show every extreme that they name: For each t and c the 12 entries act_rows[t, c, :] are distinct. `col_owner`: some owner holds exactly 24 block columns and no owner holds more.
All inputs are finite; a program needn't handle non-finite values.
Results may differ from a plain program's by a relative error of at most 0.0003.
Values may be sent and summed in bfloat16 or wider, within the bound.
A program may use at most 192 MiB of HBM per device.

v0:
```python
import jax
import jax.numpy as jnp
from jax import lax
from jax.sharding import PartitionSpec as P

D = 8192
BS = 128


epsilon = 1e-06


def on_device(hidden, out_grad, act_rows, col_owner):
    owners_count = lax.axis_size("blk")
    owner_index = lax.axis_index("blk")
    column_blocks = D // BS
    capacity = min(3 * column_blocks // (2 * owners_count), 3 * column_blocks // 4)
    per_column = act_rows.shape[2]
    owners = jnp.arange(owners_count, dtype=jnp.int32)
    onehot = (col_owner[:, None] == owners[None, :]).astype(jnp.int32)
    column_rank = jnp.sum((jnp.cumsum(onehot, axis=0) - onehot) * onehot, axis=1)
    slot_ids = jnp.arange(capacity, dtype=jnp.int32)
    matches = (col_owner[None, None, :] == owners[:, None, None]) & (
        column_rank[None, None, :] == slot_ids[None, :, None]
    )
    owned_all = jnp.sum(
        matches.astype(jnp.int32) * jnp.arange(column_blocks, dtype=jnp.int32)[None, None, :],
        axis=2,
    )
    alive_all = jnp.any(matches, axis=2)
    owned_mine = lax.dynamic_index_in_dim(owned_all, owner_index, 0, keepdims=False)
    alive_mine = lax.dynamic_index_in_dim(alive_all, owner_index, 0, keepdims=False)
    block_rows = jnp.take(act_rows[0], owned_mine, axis=0).reshape(-1)
    grad_full = lax.all_gather(out_grad, "team", axis=1, tiled=True)
    grad_mask = alive_mine.astype(jnp.bfloat16)[None, :, None]
    hidden_piece = lax.all_gather(hidden, "blk", axis=0, tiled=True)
    grad_piece = lax.all_gather(grad_full, "blk", axis=0, tiled=True)
    count_rows = grad_piece.shape[0]
    picked_grad = (
        jnp.take(grad_piece.reshape(count_rows, column_blocks, BS), owned_mine, axis=1) * grad_mask
    )
    count_rows = hidden_piece.shape[0]
    hidden_blocks = hidden_piece.reshape(count_rows, -1, BS)
    picked_hidden = jnp.take(hidden_blocks, block_rows, axis=1).reshape(
        count_rows, capacity, per_column, BS
    )
    partial_value = jnp.einsum(
        "ncki,ncj->ckij", picked_hidden, picked_grad, preferred_element_type=jnp.float32
    )
    partial_value = partial_value.reshape(capacity * per_column, BS, BS)
    gradients = lax.psum_scatter(partial_value, "dp", scatter_dimension=0, tiled=True)
    scores = jnp.sqrt(jnp.mean(gradients * gradients, axis=(1, 2)) + epsilon)
    return (gradients[None, None], scores[None, None])


def solution(mesh):
    in_specs = (P(("blk", "dp"), "team"), P(("blk", "dp"), "team"), P("team", None, None), P())
    out_specs = (P("team", "blk", "dp", None, None), P("team", "blk", "dp"))
    return jax.shard_map(
        on_device, mesh=mesh, in_specs=in_specs, out_specs=out_specs, check_vma=False
    )
```

profile of v0, /device:TPU:0, one launch (start us, length us, event | category | flops | bytes accessed | tf_op | source)
XLA Modules:
  0.0 305.4 jit_solution(6852745690831261006)
XLA Ops:
  7.2 0.0 copy-start.1
  7.2 0.0 copy-start
  7.2 0.0 all-gather.6.cloned.1.call-start
  7.2 2.0 copy.20
  9.3 0.0 all-gather.6.cloned.1.call-update
  9.3 0.0 all-gather.4.cloned.1.call-start
  9.3 3.9 %copy.17 = bf16[128,7168]{0,1:T(8,128)(2,1)} copy(bf16[128,7168]{1,0:T(8,128)(2,1)} %param.4) | data formatting | bytes 3670016 | tf_op args[0]
  13.2 0.0 all-gather.4.cloned.1.call-update
  13.2 0.0 all-gather.8.cloned.1.call-start
  13.3 44.7 %all-gather.6.cloned.1.call-done = bf16[128,8192]{0,1:T(8,128)(2,1)} async-done(((bf16[128,2048]{0,1:T(8,128)(2,1)}), bf16[128,8192]{0,1:T(8,128)(2,1)}) %all-gather.6.cloned.1.call-update) | async-done | bytes 2097168 | tf_op jit(solution)/shard_map/all_gather | solution.py:34
  58.0 0.0 all-gather.8.cloned.1.call-update
  58.0 0.0 reduce-scatter.2.cloned.1.call-start
  58.1 0.0 copy-done.1
  58.1 0.1 fusion.11
  58.1 0.1 reduce_window_sum.11
  58.2 0.0 copy-done
  58.2 0.1 copy.16
  58.3 0.2 select_reduce_fusion
  58.5 0.1 fusion.10
  58.7 0.6 gather_fusion
  59.3 0.1 compare_and_fusion
  59.4 0.1 select_n.73
  59.5 0.2 and_reduce_fusion
  59.7 78.1 %all-gather.4.cloned.1.call-done = bf16[512,7168]{0,1:T(8,128)(2,1)} async-done(((bf16[128,7168]{0,1:T(8,128)(2,1)}), bf16[512,7168]{0,1:T(8,128)(2,1)}) %all-gather.4.cloned.1.call-update) | async-done | bytes 7340048 | tf_op jit(solution)/shard_map/all_gather | solution.py:36
  137.8 10.4 %copy.18 = bf16[512,56,128]{2,0,1:T(8,128)(2,1)} copy(bf16[512,56,128]{0,2,1:T(8,128)(2,1)} %bitcast.28) | data formatting | bytes 14680064 | tf_op jit(solution)/shard_map/reshape | solution.py:43
  148.3 18.8 %gather_fusion.1 = bf16[288,512,128]{2,1,0:T(8,128)(2,1)} fusion(bf16[512,56,128]{2,0,1:T(8,128)(2,1)} %copy.18, s32[1024]{0:T(1024)S(1)} %pad_clamp_fusion), kind=kCustom, calls=%fused_computation.1 | custom fusion | bytes 75498624 | tf_op jit(solution)/shard_map/jit(_take)/gather | solution.py:44
  167.0 48.7 %copy.19 = bf16[512,24,12,128]{0,3,2,1:T(8,128)(2,1)} copy(bf16[512,24,12,128]{3,0,2,1:T(8,128)(2,1)} %bitcast.24) | data formatting | bytes 75497472 | tf_op jit(solution)/shard_map/jit(_take)/gather | solution.py:44
  215.8 11.3 %all-gather.8.cloned.1.call-done = bf16[512,8192]{0,1:T(8,128)(2,1)} async-done(((bf16[128,8192]{0,1:T(8,128)(2,1)}), bf16[512,8192]{0,1:T(8,128)(2,1)}) %all-gather.8.cloned.1.call-update) | async-done | bytes 8388624 | tf_op jit(solution)/shard_map/all_gather | solution.py:37
  227.0 11.9 %copy.21 = bf16[512,64,128]{2,0,1:T(8,128)(2,1)} copy(bf16[512,64,128]{0,2,1:T(8,128)(2,1)} %bitcast.27) | data formatting | bytes 16777216 | tf_op jit(solution)/shard_map/reshape | solution.py:40
  238.9 4.5 %gather_fusion.2 = bf16[24,512,128]{2,1,0:T(8,128)(2,1)S(1)} fusion(bf16[512,64,128]{2,0,1:T(8,128)(2,1)} %copy.21, s32[1024]{0:T(1024)S(1)} %pad_clamp_fusion.1), kind=kCustom, calls=%fused_computation.2 | custom fusion | bytes 6291552 | tf_op jit(solution)/shard_map/jit(_take)/gather | solution.py:40
  243.5 23.4 %fusion = f32[24,12,128,128]{3,2,1,0:T(8,128)} fusion(bf16[512,24,12,128]{0,3,2,1:T(8,128)(2,1)} %copy.19, pred[24,12]{1,0:T(8,128)(4,1)S(1)} %get-tuple-element.2, bf16[24,512,128]{2,1,0:T(8,128)(2,1)S(1)} %gather_fusion.2, pred[24]{0:T(512)(128)(4,1)S(1)} %compare_and_fusion.1, bf16[24]{0:T(256)(128)(2,1)S(1)} %fusion.13), kind=kOutput, calls=%fused_computation.3 | convolution fusion | flops 4853858304 | bytes 59769192 | tf_op jit(solution)/shard_map/ncki,ncj->ckij/dot_general | solution.py:47
  266.8 0.0 reduce-scatter.2.cloned.1.call-update
  266.9 26.7 %reduce-scatter.2.cloned.1.call-done = f32[144,128,128]{2,1,0:T(8,128)} async-done(((f32[288,128,128]{2,1,0:T(8,128)}), f32[144,128,128]{2,1,0:T(8,128)}) %reduce-scatter.2.cloned.1.call-update) | async-done | bytes 9437200 | tf_op jit(solution)/shard_map/reduce_scatter | solution.py:51
  293.6 4.7 %multiply_reduce_fusion = f32[144]{0:T(256)S(1)} fusion(f32[144,128,128]{2,1,0:T(8,128)} %reduce-scatter.2.cloned.1.call-done), kind=kLoop, calls=%fused_computation.7 | loop fusion | flops 4718448 | bytes 9437760 | tf_op jit(solution)/shard_map/reduce_sum | solution.py:52
  298.3 0.6 add_sqrt_fusion
  (8 shorter events, 0.1 us)
Async XLA Ops:
  7.2 50.9 %copy-start.1 = (s32[64]{0:T(128)S(1)}, s32[64]{0:T(128)}, u32[]{:S(2)}) copy-start(s32[64]{0:T(128)} %param.7) | copy-start | bytes 772
  7.2 51.1 %copy-start = (s32[1,64,12]{1,0,2:T(1,128)S(1)}, s32[1,64,12]{1,0,2:T(1,128)}, u32[]{:S(2)}) copy-start(s32[1,64,12]{1,0,2:T(1,128)} %param.6) | copy-start | bytes 9220
  7.2 50.8 %all-gather.6.cloned.1.call-start = ((), (), s32[]{:S(2)}) async-start(), calls=%async_computation.2 | async-start | bytes 2621440 | tf_op jit(solution)/shard_map/all_gather | solution.py:34
  9.3 128.5 %all-gather.4.cloned.1.call-start = ((), (), s32[]{:S(2)}) async-start(), calls=%async_computation.1 | async-start | bytes 9175040 | tf_op jit(solution)/shard_map/all_gather | solution.py:36
  13.2 213.8 %all-gather.8.cloned.1.call-start = ((), (), s32[]{:S(2)}) async-start(), calls=%async_computation.3 | async-start | bytes 10485760 | tf_op jit(solution)/shard_map/all_gather | solution.py:37
  58.0 235.6 %reduce-scatter.2.cloned.1.call-start = ((), (), s32[]{:S(2)}) async-start(), calls=%async_computation.4 | async-start | bytes 28311552 | tf_op jit(solution)/shard_map/reduce_scatter | solution.py:51
Sparse Core Ops, SparseCore 0:
  9.6 48.3 all-gather.5
  60.4 77.4 all-gather.3
  139.7 87.3 all-gather.7
  267.0 26.5 reduce-scatter.1
where the time goes:
time: 307 us; the launch traced here: 305 us
  waiting for transfers between devices  161 us (52%)
  local copies, waits for them, and re-layouts  101 us (33%)
  matrix products  23.4 us (8%)
  between operations  13.9 us (5%)
  other arithmetic  6.12 us (2%)
    all_gather x1, waiting for transfers between devices, on_device(): hidden_piece = lax.all_gather(hidden, 'blk', axis=0, tiled=True)  78.1 us
    gather x2, local copies, waits for them, and re-layouts, on_device(): jnp.take(hidden_blocks, block_rows, axis=1)  67.5 us
    all_gather x1, waiting for transfers between devices, on_device(): grad_full = lax.all_gather(out_grad, 'team', axis=1, tiled=True)  44.7 us
    reduce_scatter x1, waiting for transfers between devices, on_device(): lax.psum_scatter(partial_value, 'dp', scatter_dimension=0, tiled=True)  26.7 us
    dot_general x1, matrix products, on_device(): jnp.einsum('ncki,ncj->ckij', picked_hidden, picked_grad, preferred_elemen...  23.4 us
    reshape x1, local copies, waits for them, and re-layouts, on_device(): grad_piece.reshape(count_rows, column_blocks, BS)  11.9 us
    all_gather x1, waiting for transfers between devices, on_device(): grad_piece = lax.all_gather(grad_full, 'blk', axis=0, tiled=True)  11.3 us
    reshape x1, local copies, waits for them, and re-layouts, on_device(): hidden_blocks = hidden_piece.reshape(count_rows, -1, BS)  10.4 us
  transfers between devices with their start and end apart: 4, of which 4 were waited for; matrix products, arithmetic and copies ran while one was open for 27% of the time, Pallas kernels for 0%

commit v1 on v0

--- a/solution.py
+++ b/solution.py
@@ -1,21 +1,22 @@
+import functools
+
 import jax
 import jax.numpy as jnp
 from jax import lax
+from jax.experimental import pallas as pl
+from jax.experimental.pallas import tpu as pltpu
 from jax.sharding import PartitionSpec as P
 
-D = 8192
 BS = 128
+MESH = pl.DeviceIdType.MESH
+CHUNKS = 4
 
 
 epsilon = 1e-06
 
 
-def on_device(hidden, out_grad, act_rows, col_owner):
-    owners_count = lax.axis_size("blk")
-    owner_index = lax.axis_index("blk")
-    column_blocks = D // BS
-    capacity = min(3 * column_blocks // (2 * owners_count), 3 * column_blocks // 4)
-    per_column = act_rows.shape[2]
+def owner_tables(col_owner, owners_count, capacity):
+    column_blocks = col_owner.shape[0]
     owners = jnp.arange(owners_count, dtype=jnp.int32)
     onehot = (col_owner[:, None] == owners[None, :]).astype(jnp.int32)
     column_rank = jnp.sum((jnp.cumsum(onehot, axis=0) - onehot) * onehot, axis=1)
@@ -27,7 +28,313 @@
         matches.astype(jnp.int32) * jnp.arange(column_blocks, dtype=jnp.int32)[None, None, :],
         axis=2,
     )
-    alive_all = jnp.any(matches, axis=2)
+    return owned_all, jnp.any(matches, axis=2)
+
+
+def gather_kernel(
+    cols_ref, hid_ref, grad_ref, hfull, gfull, gz, gcol, snd, send_sem, recv_sem, local_sem
+):
+    teams = lax.axis_size("team")
+    b, t, d = lax.axis_index("blk"), lax.axis_index("team"), lax.axis_index("dp")
+    y, x = b // 2, b % 2
+    panels, panel_rows, _ = hfull.shape
+    part_rows = panel_rows // teams
+    part_cols = grad_ref.shape[1]
+    picks = cols_ref.shape[1]
+    chunk = panel_rows // CHUNKS
+
+    def plane(sy, sx, sd):
+        oy = 1 - y if sy else y
+        ox = 1 - x if sx else x
+        return oy * 2 + ox, (1 - d if sd else d)
+
+    def panel_of(sy, sx, sd):
+        ob, od = plane(sy, sx, sd)
+        return ob * 2 + od
+
+    def device(sy, sx, sd):
+        ob, od = plane(sy, sx, sd)
+        return (ob, t, od)
+
+    mine = panel_of(0, 0, 0)
+    flips = [(sy, sx, sd) for sy in (0, 1) for sx in (0, 1) for sd in (0, 1)][1:]
+
+    barrier = pltpu.get_barrier_semaphore()
+    for flip in flips:
+        pl.semaphore_signal(barrier, inc=1, device_id=device(*flip), device_id_type=MESH)
+    for s in range(1, teams):
+        pl.semaphore_signal(
+            barrier, inc=1, device_id=(b, (t + s) % teams, d), device_id_type=MESH
+        )
+    pl.semaphore_wait(barrier, len(flips) + teams - 1)
+
+    counter = [0]
+
+    def remote(src, dst, target, slot=None):
+        if slot is None:
+            slot = counter[0]
+            counter[0] += 1
+        return pltpu.make_async_remote_copy(
+            src_ref=src,
+            dst_ref=dst,
+            send_sem=send_sem.at[slot],
+            recv_sem=recv_sem.at[slot],
+            device_id=target,
+            device_id_type=MESH,
+        )
+
+    sent = []
+
+    def rows_of(c):
+        return pl.ds(c * chunk, chunk)
+
+    def send_own(flip, c):
+        copy = remote(hid_ref.at[rows_of(c)], hfull.at[mine, rows_of(c)], device(*flip))
+        copy.start()
+        sent.append(copy)
+        return copy
+
+    def forward(panel, flip, c):
+        piece = hfull.at[panel, rows_of(c)]
+        copy = remote(piece, piece, device(*flip))
+        copy.start()
+        sent.append(copy)
+        return copy
+
+    def part(k):
+        return pl.ds(k * part_rows, part_rows)
+
+    def quarter(k):
+        return pl.ds(k * part_cols, part_cols)
+
+    own_grad = pltpu.make_async_copy(
+        grad_ref.at[part(t)], gz.at[:, quarter(t)], local_sem.at[0]
+    )
+    stage1 = []
+    for s in range(1, teams):
+        target = (t + s) % teams
+        copy = remote(grad_ref.at[part(target)], gz.at[:, quarter(t)], (b, target, d))
+        copy.start()
+        stage1.append(copy)
+        sent.append(copy)
+    own_grad.start()
+
+    order_x = list(range(CHUNKS))
+    order_y = order_x[CHUNKS // 2 :] + order_x[: CHUNKS // 2]
+    X, Y, SIB = (0, 1, 0), (1, 0, 0), (0, 0, 1)
+    from_x, from_y, from_sib = {}, {}, []
+    from_x[order_x[0]] = send_own(X, order_x[0])
+    from_y[order_y[0]] = send_own(Y, order_y[0])
+    own_hidden = pltpu.make_async_copy(hid_ref, hfull.at[mine], local_sem.at[1])
+    own_hidden.start()
+
+    own_grad.wait()
+    for copy in stage1:
+        copy.wait_recv()
+
+    for c in range(gcol.shape[0]):
+        gcol[c] = gz[:, c * BS : (c + 1) * BS]
+
+    def pick(p, carry):
+        for j in range(picks):
+            snd[p, :, j * BS : (j + 1) * BS] = gcol[cols_ref[p, j]]
+        return carry
+
+    lax.fori_loop(0, panels, pick, 0)
+    stage2 = []
+    for flip in flips:
+        copy = remote(snd.at[panel_of(*flip)], gfull.at[mine, part(t)], device(*flip))
+        copy.start()
+        stage2.append(copy)
+        sent.append(copy)
+    own_pick = pltpu.make_async_copy(snd.at[mine], gfull.at[mine, part(t)], local_sem.at[2])
+    own_pick.start()
+
+    for i in range(1, CHUNKS):
+        from_x[order_x[i]] = send_own(X, order_x[i])
+        from_y[order_y[i]] = send_own(Y, order_y[i])
+    for c in range(CHUNKS):
+        from_sib.append(send_own(SIB, c))
+
+    own_pick.wait()
+    for copy in stage2:
+        copy.wait_recv()
+
+    chain_base = counter[0]
+    counter[0] += 2 * (teams - 1)
+
+    def chain(up, k, shard, target):
+        piece = gfull.at[:, part(shard)]
+        slot = chain_base + (k if up else teams - 1 + k)
+        return remote(piece, piece, (b, target, d), slot)
+
+    def chain_send(k, wait):
+        @pl.when((t < teams - 1) & (t - k >= 0))
+        def _():
+            copy = chain(True, k, t - k, t + 1)
+            copy.wait_send() if wait else copy.start()
+
+        @pl.when((t > 0) & (t + k < teams))
+        def _():
+            copy = chain(False, k, t + k, t - 1)
+            copy.wait_send() if wait else copy.start()
+
+    def chain_recv(k):
+        @pl.when(t - 1 - k >= 0)
+        def _():
+            chain(True, k, t - 1 - k, t - 1).wait_recv()
+
+        @pl.when(t + 1 + k < teams)
+        def _():
+            chain(False, k, t + 1 + k, t + 1).wait_recv()
+
+    chain_send(0, False)
+
+    panel_x, panel_y, panel_xy = panel_of(*X), panel_of(*Y), panel_of(1, 1, 0)
+    from_xy = {}
+    steps = 0
+    for i in range(CHUNKS):
+        cx, cy = order_x[i], order_y[i]
+        from_x[cx].wait_recv()
+        if i < CHUNKS // 2:
+            from_xy[cx] = forward(panel_x, Y, cx)
+        from_sib.append(forward(panel_x, SIB, cx))
+        from_y[cy].wait_recv()
+        if i < CHUNKS // 2:
+            from_xy[cy] = forward(panel_y, X, cy)
+        from_sib.append(forward(panel_y, SIB, cy))
+        if i % 2 == 1 and steps < teams - 1:
+            chain_recv(steps)
+            steps += 1
+            if steps < teams - 1:
+                chain_send(steps, False)
+    for c in order_x:
+        c = order_x[c // 2] if c % 2 == 0 else order_y[c // 2]
+        from_xy[c].wait_recv()
+        from_sib.append(forward(panel_xy, SIB, c))
+    while steps < teams - 1:
+        chain_recv(steps)
+        steps += 1
+        if steps < teams - 1:
+            chain_send(steps, False)
+    for copy in from_sib:
+        copy.wait_recv()
+    for copy in sent:
+        copy.wait_send()
+    for k in range(teams - 1):
+        chain_send(k, True)
+    own_hidden.wait()
+
+
+def gather(columns, hidden, out_grad, panels):
+    teams = lax.axis_size("team")
+    panel_rows, units = hidden.shape
+    picks = columns.shape[1]
+    copies = (teams - 1) + 7 + 3 * CHUNKS + 4 * CHUNKS + 2 * (teams - 1)
+    hbm = pl.BlockSpec(memory_space=pl.ANY)
+    return pl.pallas_call(
+        gather_kernel,
+        out_shape=(
+            jax.ShapeDtypeStruct((panels, panel_rows, units), hidden.dtype),
+            jax.ShapeDtypeStruct((panels, panel_rows, picks * BS), out_grad.dtype),
+        ),
+        in_specs=[pl.BlockSpec(memory_space=pltpu.SMEM), hbm, hbm],
+        out_specs=(hbm, hbm),
+        scratch_shapes=[
+            pltpu.VMEM((panel_rows // teams, teams * out_grad.shape[1]), out_grad.dtype),
+            pltpu.VMEM(
+                (teams * out_grad.shape[1] // BS, panel_rows // teams, BS), out_grad.dtype
+            ),
+            pltpu.VMEM((panels, panel_rows // teams, picks * BS), out_grad.dtype),
+            pltpu.SemaphoreType.DMA((copies,)),
+            pltpu.SemaphoreType.DMA((copies,)),
+            pltpu.SemaphoreType.DMA((3,)),
+        ],
+        compiler_params=pltpu.CompilerParams(collective_id=0, has_side_effects=True),
+    )(columns, hidden, out_grad)
+
+
+def block_kernel(rows_ref, alive_ref, h_ref, g_ref, out_ref, ssq_ref):
+    j = pl.program_id(0)
+    per_column = out_ref.shape[0]
+    scale = alive_ref[j].astype(jnp.float32)
+    g_t = g_ref[...].T
+    for k in range(0, per_column, 2):
+        pair = []
+        for i in (k, k + 1):
+            r = rows_ref[j * per_column + i]
+            pair.append(h_ref[:, pl.ds(pl.multiple_of(r * BS, BS), BS)])
+        both = jnp.dot(
+            g_t, jnp.concatenate(pair, axis=1), preferred_element_type=jnp.float32
+        )
+        for i in range(2):
+            block = both[:, i * BS : (i + 1) * BS].T * scale
+            out_ref[k + i] = block
+            ssq_ref[0, k + i, :] = jnp.sum(block * block, axis=0)
+
+
+def blocks(rows, alive, hidden, grad):
+    picks = alive.shape[0]
+    per_column = rows.shape[0] // picks
+    tokens, units = hidden.shape
+    return pl.pallas_call(
+        block_kernel,
+        out_shape=(
+            jax.ShapeDtypeStruct((picks * per_column, BS, BS), jnp.float32),
+            jax.ShapeDtypeStruct((picks, per_column, BS), jnp.float32),
+        ),
+        grid_spec=pltpu.PrefetchScalarGridSpec(
+            num_scalar_prefetch=2,
+            grid=(picks,),
+            in_specs=[
+                pl.BlockSpec(
+                    (tokens, units), lambda j, *_: (0, 0), pipeline_mode=pl.Buffered(1)
+                ),
+                pl.BlockSpec((tokens, BS), lambda j, *_: (0, j)),
+            ],
+            out_specs=(
+                pl.BlockSpec((per_column, BS, BS), lambda j, *_: (j, 0, 0)),
+                pl.BlockSpec((1, per_column, BS), lambda j, *_: (j, 0, 0)),
+            ),
+        ),
+        compiler_params=pltpu.CompilerParams(dimension_semantics=("arbitrary",)),
+    )(rows, alive, hidden, grad)
+
+
+def in_plane(hidden, out_grad, act_rows, col_owner):
+    owners_count, cores = lax.axis_size("blk"), lax.axis_size("dp")
+    column_blocks = col_owner.shape[0]
+    capacity = min(3 * column_blocks // (2 * owners_count), 3 * column_blocks // 4)
+    owned_all, alive_all = owner_tables(col_owner, owners_count, capacity)
+    panels = owners_count * cores
+    picks = capacity // cores
+    columns = owned_all.reshape(panels, picks)
+    mine = lax.axis_index("blk") * cores + lax.axis_index("dp")
+    columns_mine = lax.dynamic_index_in_dim(columns, mine, 0, keepdims=False)
+    alive_mine = lax.dynamic_index_in_dim(
+        alive_all.reshape(panels, picks), mine, 0, keepdims=False
+    ).astype(jnp.int32)
+    rows = jnp.take(act_rows[0], columns_mine, axis=0).reshape(-1)
+    hidden_all, grad_mine = gather(columns, hidden, out_grad, panels)
+    tokens = panels * hidden.shape[0]
+    gradients, ssq = blocks(
+        rows,
+        alive_mine,
+        hidden_all.reshape(tokens, hidden.shape[1]),
+        grad_mine.reshape(tokens, picks * BS),
+    )
+    mean = jnp.sum(ssq, axis=2).reshape(-1) * (1.0 / (BS * BS))
+    scores = jnp.sqrt(mean + epsilon)
+    return (gradients[None, None], scores[None, None])
+
+
+def on_device(hidden, out_grad, act_rows, col_owner):
+    owners_count = lax.axis_size("blk")
+    owner_index = lax.axis_index("blk")
+    column_blocks = col_owner.shape[0]
+    capacity = min(3 * column_blocks // (2 * owners_count), 3 * column_blocks // 4)
+    per_column = act_rows.shape[2]
+    owned_all, alive_all = owner_tables(col_owner, owners_count, capacity)
     owned_mine = lax.dynamic_index_in_dim(owned_all, owner_index, 0, keepdims=False)
     alive_mine = lax.dynamic_index_in_dim(alive_all, owner_index, 0, keepdims=False)
     block_rows = jnp.take(act_rows[0], owned_mine, axis=0).reshape(-1)
@@ -39,7 +346,6 @@
     picked_grad = (
         jnp.take(grad_piece.reshape(count_rows, column_blocks, BS), owned_mine, axis=1) * grad_mask
     )
-    count_rows = hidden_piece.shape[0]
     hidden_blocks = hidden_piece.reshape(count_rows, -1, BS)
     picked_hidden = jnp.take(hidden_blocks, block_rows, axis=1).reshape(
         count_rows, capacity, per_column, BS
@@ -56,6 +362,11 @@
 def solution(mesh):
     in_specs = (P(("blk", "dp"), "team"), P(("blk", "dp"), "team"), P("team", None, None), P())
     out_specs = (P("team", "blk", "dp", None, None), P("team", "blk", "dp"))
+    square = mesh.shape["blk"] == 4 and mesh.shape["dp"] == 2
     return jax.shard_map(
-        on_device, mesh=mesh, in_specs=in_specs, out_specs=out_specs, check_vma=False
-    )
+        in_plane if square else on_device,
+        mesh=mesh,
+        in_specs=in_specs,
+        out_specs=out_specs,
+        check_vma=False,
+    )

time: 307 us -> 117 us (0.38)
  waiting for transfers between devices: 161 us -> 0 us
  Pallas kernels: 0 us -> 109 us
  local copies, waits for them, and re-layouts: 101 us -> 2.8 us
  matrix products: 23.4 us -> 0 us
  between operations: 13.9 us -> 0.7 us
    all_gather x3 -> x0, waiting for transfers between devices: 134 us -> none  [the longest x1 78.1 us: on_device(): hidden_piece = lax.all_gather(hidden, 'blk', axis=0, tiled=True)]
    pallas_call x0 -> x2, Pallas kernels: none -> 109 us  [the longest x1 87.6 us: gather(): pl.pallas_call(gather_kernel, out_shape=(jax.ShapeDtypeStruct((panels, pa...]
    gather x4 -> x1, local copies, waits for them, and re-layouts: 72.6 us -> 0.56 us  [in_plane(): rows = jnp.take(act_rows[0], columns_mine, axis=0).reshape(-1)]
    reduce_scatter x1 -> x0, waiting for transfers between devices: 26.7 us -> none  [on_device(): lax.psum_scatter(partial_value, 'dp', scatter_dimension=0, tiled=True)]
    dot_general x1 -> x0, matrix products: 23.4 us -> none  [on_device(): jnp.einsum('ncki,ncj->ckij', picked_hidden, picked_grad, preferred_elemen...]
    reshape x2, local copies, waits for them, and re-layouts: 22.3 us -> 0.16 us  [the longest x1 0.08 us: in_plane(): alive_all.reshape(panels, picks)]
    unnamed x7 -> x3, local copies, waits for them, and re-layouts: 6.01 us -> 0.78 us
    reduce_sum x3, other arithmetic: 5.05 us -> 1.98 us  [the longest x1 0.99 us: in_plane(): mean = jnp.sum(ssq, axis=2).reshape(-1) * (1.0 / (BS * BS))]
  transfers between devices with their start and end apart: 4 -> 0, of which waited for: 4 -> 0; matrix products, arithmetic and copies ran while one was open for 27% -> 0% of each run, Pallas kernels for 0% -> 0%
where the time goes in v1:
time: 117 us
  Pallas kernels  109 us (93%)
  other arithmetic  4.27 us (4%)
  local copies, waits for them, and re-layouts  2.8 us (2%)
    pallas_call x1, Pallas kernels, gather(): pl.pallas_call(gather_kernel, out_shape=(jax.ShapeDtypeStruct((panels, pa...  87.6 us
    pallas_call x1, Pallas kernels, blocks(): pl.pallas_call(block_kernel, out_shape=(jax.ShapeDtypeStruct((picks * per...  21.3 us

profile of v1, /device:TPU:0, one launch (start us, length us, event | category | flops | bytes accessed | tf_op | source)
XLA Modules:
  0.0 116.6 jit_solution(13723584747458228749)
XLA Ops:
  0.6 0.7 iota_compare_fusion.2
  1.3 0.8 copy.7
  2.1 0.7 fusion.1
  2.8 0.1 reduce_window_sum.11
  2.9 0.8 select_reduce_fusion
  3.8 0.2 and_reduce_fusion
  3.9 0.2 fusion
  4.1 0.1 reshape.127
  4.2 0.5 fusion.2.alive_ref
  4.7 0.1 reshape.126.cols_ref
  4.8 0.0 copy-start
  4.8 0.6 gather_fusion
  5.4 0.1 broadcast_select_fusion
  5.4 0.7 select_n.34.rows_ref
  6.1 0.0 copy-done
  6.1 87.6 %shard_map.59 = (bf16[8,128,7168]{2,1,0:T(8,128)(2,1)}, bf16[8,128,1536]{2,1,0:T(8,128)(2,1)}) custom-call(s32[8,12]{1,0:T(8,128)} %copy-done, bf16[128,7168]{1,0:T(8,128)(2,1)} %hid_ref.1, bf16[128,2048]{1,0:T(8,128)(2,1)} %grad_ref.1), custom_call_target="tpu_custom_call" | custom-call | tf_op jit(solution)/shard_map/pallas_call | solution.py:235
  93.7 21.3 %shard_map.60 = (f32[144,128,128]{2,1,0:T(8,128)}, f32[12,12,128]{2,1,0:T(8,128)}) custom-call(s32[144]{0:T(256)} %select_n.34.rows_ref, s32[12]{0:T(128)} %fusion.2.alive_ref, bf16[1024,7168]{1,0:T(8,128)(2,1)} %bitcast.12, bf16[1024,1536]{1,0:T(8,128)(2,1)} %bitcast.13), custom_call_target="tpu_custom_call" | custom-call | tf_op jit(solution)/shard_map/pallas_call | solution.py:280
  114.9 1.0 reduce_sum.29
  116.0 0.6 sqrt.14
  (5 shorter events, 0.0 us)
Async XLA Ops:
  4.8 1.3 %copy-start = (s32[8,12]{1,0:T(8,128)}, s32[8,12]{1,0:T(8,128)S(1)}, u32[]{:S(2)}) copy-start(s32[8,12]{1,0:T(8,128)S(1)} %reshape.126.cols_ref) | copy-start | bytes 1156

commit v2 on v1

--- a/solution.py
+++ b/solution.py
@@ -32,16 +32,35 @@
 
 
 def gather_kernel(
-    cols_ref, hid_ref, grad_ref, hfull, gfull, gz, gcol, snd, send_sem, recv_sem, local_sem
+    cols_ref,
+    rows_ref,
+    hid_ref,
+    grad_ref,
+    sums_ref,
+    far_ref,
+    far_grad,
+    near,
+    sums,
+    gfull,
+    gz,
+    gcol,
+    snd,
+    send_sem,
+    recv_sem,
+    local_sem,
+    block_sem,
+    sums_sem,
 ):
     teams = lax.axis_size("team")
     b, t, d = lax.axis_index("blk"), lax.axis_index("team"), lax.axis_index("dp")
     y, x = b // 2, b % 2
-    panels, panel_rows, _ = hfull.shape
+    panels, panel_rows, _ = gfull.shape
+    units = near.shape[0]
+    near_panels = near.shape[1] // panel_rows
     part_rows = panel_rows // teams
     part_cols = grad_ref.shape[1]
     picks = cols_ref.shape[1]
-    chunk = panel_rows // CHUNKS
+    chunk = units // CHUNKS
 
     def plane(sy, sx, sd):
         oy = 1 - y if sy else y
@@ -56,8 +75,21 @@
         ob, od = plane(sy, sx, sd)
         return (ob, t, od)
 
+    def slot_of(flip):
+        return (flip[0] * 2 + flip[1]) * 2 + flip[2]
+
     mine = panel_of(0, 0, 0)
     flips = [(sy, sx, sd) for sy in (0, 1) for sx in (0, 1) for sd in (0, 1)][1:]
+
+    own_blocks = [
+        pltpu.make_async_copy(
+            hid_ref.at[:, pl.ds(r * BS, BS)],
+            near.at[r, pl.ds(0, panel_rows)],
+            block_sem.at[r],
+        )
+        for r in range(units)
+    ]
+    own_ready = set()
 
     barrier = pltpu.get_barrier_semaphore()
     for flip in flips:
@@ -85,21 +117,25 @@
 
     sent = []
 
-    def rows_of(c):
-        return pl.ds(c * chunk, chunk)
-
-    def send_own(flip, c):
-        copy = remote(hid_ref.at[rows_of(c)], hfull.at[mine, rows_of(c)], device(*flip))
+    def piece(slot, c):
+        held = pl.ds(c * chunk, chunk)
+        if slot < near_panels:
+            return near.at[held, pl.ds(slot * panel_rows, panel_rows)]
+        return far_ref.at[held, pl.ds((slot - near_panels) * panel_rows, panel_rows)]
+
+    def forward(source, flip, c):
+        there = tuple(one ^ two for one, two in zip(source, flip))
+        copy = remote(piece(slot_of(source), c), piece(slot_of(there), c), device(*flip))
         copy.start()
         sent.append(copy)
         return copy
 
-    def forward(panel, flip, c):
-        piece = hfull.at[panel, rows_of(c)]
-        copy = remote(piece, piece, device(*flip))
-        copy.start()
-        sent.append(copy)
-        return copy
+    def send_own(flip, c):
+        if c not in own_ready:
+            own_ready.add(c)
+            for r in range(c * chunk, (c + 1) * chunk):
+                own_blocks[r].wait()
+        return forward((0, 0, 0), flip, c)
 
     def part(k):
         return pl.ds(k * part_rows, part_rows)
@@ -119,14 +155,16 @@
         sent.append(copy)
     own_grad.start()
 
+    X, Y, XY, SIB = (0, 1, 0), (1, 0, 0), (1, 1, 0), (0, 0, 1)
     order_x = list(range(CHUNKS))
     order_y = order_x[CHUNKS // 2 :] + order_x[: CHUNKS // 2]
-    X, Y, SIB = (0, 1, 0), (1, 0, 0), (0, 0, 1)
+    for pair in zip(order_x[: CHUNKS // 2], order_y[: CHUNKS // 2]):
+        for c in pair:
+            for r in range(c * chunk, (c + 1) * chunk):
+                own_blocks[r].start()
     from_x, from_y, from_sib = {}, {}, []
     from_x[order_x[0]] = send_own(X, order_x[0])
     from_y[order_y[0]] = send_own(Y, order_y[0])
-    own_hidden = pltpu.make_async_copy(hid_ref, hfull.at[mine], local_sem.at[1])
-    own_hidden.start()
 
     own_grad.wait()
     for copy in stage1:
@@ -143,11 +181,11 @@
     lax.fori_loop(0, panels, pick, 0)
     stage2 = []
     for flip in flips:
-        copy = remote(snd.at[panel_of(*flip)], gfull.at[mine, part(t)], device(*flip))
+        copy = remote(snd.at[panel_of(*flip)], gfull.at[slot_of(flip), part(t)], device(*flip))
         copy.start()
         stage2.append(copy)
         sent.append(copy)
-    own_pick = pltpu.make_async_copy(snd.at[mine], gfull.at[mine, part(t)], local_sem.at[2])
+    own_pick = pltpu.make_async_copy(snd.at[mine], gfull.at[0, part(t)], local_sem.at[2])
     own_pick.start()
 
     for i in range(1, CHUNKS):
@@ -164,9 +202,9 @@
     counter[0] += 2 * (teams - 1)
 
     def chain(up, k, shard, target):
-        piece = gfull.at[:, part(shard)]
+        subset = gfull.at[:, part(shard)]
         slot = chain_base + (k if up else teams - 1 + k)
-        return remote(piece, piece, (b, target, d), slot)
+        return remote(subset, subset, (b, target, d), slot)
 
     def chain_send(k, wait):
         @pl.when((t < teams - 1) & (t - k >= 0))
@@ -190,57 +228,95 @@
 
     chain_send(0, False)
 
-    panel_x, panel_y, panel_xy = panel_of(*X), panel_of(*Y), panel_of(1, 1, 0)
     from_xy = {}
     steps = 0
     for i in range(CHUNKS):
         cx, cy = order_x[i], order_y[i]
         from_x[cx].wait_recv()
         if i < CHUNKS // 2:
-            from_xy[cx] = forward(panel_x, Y, cx)
-        from_sib.append(forward(panel_x, SIB, cx))
+            from_xy[cx] = forward(X, Y, cx)
+        from_sib.append(forward(X, SIB, cx))
         from_y[cy].wait_recv()
         if i < CHUNKS // 2:
-            from_xy[cy] = forward(panel_y, X, cy)
-        from_sib.append(forward(panel_y, SIB, cy))
+            from_xy[cy] = forward(Y, X, cy)
+        from_sib.append(forward(Y, SIB, cy))
         if i % 2 == 1 and steps < teams - 1:
             chain_recv(steps)
             steps += 1
             if steps < teams - 1:
                 chain_send(steps, False)
-    for c in order_x:
-        c = order_x[c // 2] if c % 2 == 0 else order_y[c // 2]
+    arrivals = [c for pair in zip(order_x[: CHUNKS // 2], order_y[: CHUNKS // 2]) for c in pair]
+
+    def pass_on(c):
         from_xy[c].wait_recv()
-        from_sib.append(forward(panel_xy, SIB, c))
+        from_far.append(forward(XY, SIB, c))
+
+    from_far = []
+    for c in arrivals[: CHUNKS // 2]:
+        pass_on(c)
     while steps < teams - 1:
         chain_recv(steps)
         steps += 1
         if steps < teams - 1:
             chain_send(steps, False)
+    give_grad = pltpu.make_async_copy(
+        gfull.at[pl.ds(near_panels, panels - near_panels)], far_grad, local_sem.at[1]
+    )
+    give_grad.start()
     for copy in from_sib:
+        copy.wait_recv()
+
+    pairs = sums.shape[1]
+
+    def give_sums(j):
+        return pltpu.make_async_copy(sums.at[j], sums_ref.at[j], sums_sem.at[j])
+
+    def column(j, carry):
+        lanes = pl.ds(pl.multiple_of(j * BS, BS), BS)
+        g_t = gfull[:near_panels, :, lanes].reshape(near_panels * panel_rows, BS).T
+        for k in range(pairs):
+            s = (j * pairs + k) * 2
+            both = jnp.concatenate([near[rows_ref[s]], near[rows_ref[s + 1]]], axis=1)
+            sums[j, k] = jnp.dot(g_t, both, preferred_element_type=jnp.float32)
+        give_sums(j).start()
+        return carry
+
+    lax.fori_loop(0, picks, column, 0)
+    for c in arrivals[CHUNKS // 2 :]:
+        pass_on(c)
+    for copy in from_far:
         copy.wait_recv()
     for copy in sent:
         copy.wait_send()
     for k in range(teams - 1):
         chain_send(k, True)
-    own_hidden.wait()
-
-
-def gather(columns, hidden, out_grad, panels):
+    give_grad.wait()
+    for j in range(picks):
+        give_sums(j).wait()
+
+
+def gather(columns, rows, hidden, out_grad, panels):
     teams = lax.axis_size("team")
     panel_rows, units = hidden.shape
     picks = columns.shape[1]
+    pairs = rows.shape[0] // picks // 2
+    near, far = panels - 2, 2
     copies = (teams - 1) + 7 + 3 * CHUNKS + 4 * CHUNKS + 2 * (teams - 1)
     hbm = pl.BlockSpec(memory_space=pl.ANY)
+    smem = pl.BlockSpec(memory_space=pltpu.SMEM)
     return pl.pallas_call(
         gather_kernel,
         out_shape=(
-            jax.ShapeDtypeStruct((panels, panel_rows, units), hidden.dtype),
-            jax.ShapeDtypeStruct((panels, panel_rows, picks * BS), out_grad.dtype),
+            jax.ShapeDtypeStruct((picks, pairs, BS, 2 * BS), jnp.float32),
+            jax.ShapeDtypeStruct((units // BS, far * panel_rows, BS), hidden.dtype),
+            jax.ShapeDtypeStruct((far, panel_rows, picks * BS), out_grad.dtype),
         ),
-        in_specs=[pl.BlockSpec(memory_space=pltpu.SMEM), hbm, hbm],
-        out_specs=(hbm, hbm),
+        in_specs=[smem, smem, hbm, hbm],
+        out_specs=(hbm, hbm, hbm),
         scratch_shapes=[
+            pltpu.VMEM((units // BS, near * panel_rows, BS), hidden.dtype),
+            pltpu.VMEM((picks, pairs, BS, 2 * BS), jnp.float32),
+            pltpu.VMEM((panels, panel_rows, picks * BS), out_grad.dtype),
             pltpu.VMEM((panel_rows // teams, teams * out_grad.shape[1]), out_grad.dtype),
             pltpu.VMEM(
                 (teams * out_grad.shape[1] // BS, panel_rows // teams, BS), out_grad.dtype
@@ -249,34 +325,32 @@
             pltpu.SemaphoreType.DMA((copies,)),
             pltpu.SemaphoreType.DMA((copies,)),
             pltpu.SemaphoreType.DMA((3,)),
+            pltpu.SemaphoreType.DMA((units // BS,)),
+            pltpu.SemaphoreType.DMA((picks,)),
         ],
         compiler_params=pltpu.CompilerParams(collective_id=0, has_side_effects=True),
-    )(columns, hidden, out_grad)
-
-
-def block_kernel(rows_ref, alive_ref, h_ref, g_ref, out_ref, ssq_ref):
+    )(columns, rows, hidden, out_grad)
+
+
+def block_kernel(rows_ref, alive_ref, sums_ref, h_ref, g_ref, out_ref, ssq_ref):
     j = pl.program_id(0)
     per_column = out_ref.shape[0]
     scale = alive_ref[j].astype(jnp.float32)
     g_t = g_ref[...].T
     for k in range(0, per_column, 2):
-        pair = []
-        for i in (k, k + 1):
-            r = rows_ref[j * per_column + i]
-            pair.append(h_ref[:, pl.ds(pl.multiple_of(r * BS, BS), BS)])
-        both = jnp.dot(
-            g_t, jnp.concatenate(pair, axis=1), preferred_element_type=jnp.float32
-        )
+        s = j * per_column + k
+        pair = jnp.concatenate([h_ref[rows_ref[s]], h_ref[rows_ref[s + 1]]], axis=1)
+        both = sums_ref[0, k // 2] + jnp.dot(g_t, pair, preferred_element_type=jnp.float32)
         for i in range(2):
             block = both[:, i * BS : (i + 1) * BS].T * scale
             out_ref[k + i] = block
             ssq_ref[0, k + i, :] = jnp.sum(block * block, axis=0)
 
 
-def blocks(rows, alive, hidden, grad):
-    picks = alive.shape[0]
-    per_column = rows.shape[0] // picks
-    tokens, units = hidden.shape
+def blocks(rows, alive, sums, hidden, grad):
+    picks, pairs = sums.shape[:2]
+    per_column = pairs * 2
+    tokens = grad.shape[0]
     return pl.pallas_call(
         block_kernel,
         out_shape=(
@@ -287,8 +361,9 @@
             num_scalar_prefetch=2,
             grid=(picks,),
             in_specs=[
+                pl.BlockSpec((1, pairs, BS, 2 * BS), lambda j, *_: (j, 0, 0, 0)),
                 pl.BlockSpec(
-                    (tokens, units), lambda j, *_: (0, 0), pipeline_mode=pl.Buffered(1)
+                    hidden.shape, lambda j, *_: (0, 0, 0), pipeline_mode=pl.Buffered(1)
                 ),
                 pl.BlockSpec((tokens, BS), lambda j, *_: (0, j)),
             ],
@@ -298,7 +373,7 @@
             ),
         ),
         compiler_params=pltpu.CompilerParams(dimension_semantics=("arbitrary",)),
-    )(rows, alive, hidden, grad)
+    )(rows, alive, sums, hidden, grad)
 
 
 def in_plane(hidden, out_grad, act_rows, col_owner):
@@ -315,13 +390,9 @@
         alive_all.reshape(panels, picks), mine, 0, keepdims=False
     ).astype(jnp.int32)
     rows = jnp.take(act_rows[0], columns_mine, axis=0).reshape(-1)
-    hidden_all, grad_mine = gather(columns, hidden, out_grad, panels)
-    tokens = panels * hidden.shape[0]
+    sums, far_hidden, far_grad = gather(columns, rows, hidden, out_grad, panels)
     gradients, ssq = blocks(
-        rows,
-        alive_mine,
-        hidden_all.reshape(tokens, hidden.shape[1]),
-        grad_mine.reshape(tokens, picks * BS),
+        rows, alive_mine, sums, far_hidden, far_grad.reshape(-1, picks * BS)
     )
     mean = jnp.sum(ssq, axis=2).reshape(-1) * (1.0 / (BS * BS))
     scores = jnp.sqrt(mean + epsilon)

time: 117 us -> 119 us (1.017)
  Pallas kernels: 109 us -> 111 us
    pallas_call x1, Pallas kernels: 87.6 us -> 95.6 us  [gather(): pl.pallas_call(gather_kernel, out_shape=(jax.ShapeDtypeStruct((picks, pai...]
    pallas_call x1, Pallas kernels: 21.3 us -> 15 us  [blocks(): pl.pallas_call(block_kernel, out_shape=(jax.ShapeDtypeStruct((picks * per...]
where the time goes in v2:
time: 119 us; the launch traced here: 118 us
  Pallas kernels  111 us (93%)
  other arithmetic  4.23 us (4%)
  local copies, waits for them, and re-layouts  2.8 us (2%)
    pallas_call x1, Pallas kernels, gather(): pl.pallas_call(gather_kernel, out_shape=(jax.ShapeDtypeStruct((picks, pai...  95.6 us
    pallas_call x1, Pallas kernels, blocks(): pl.pallas_call(block_kernel, out_shape=(jax.ShapeDtypeStruct((picks * per...  15 us

profile of v2, /device:TPU:0, one launch (start us, length us, event | category | flops | bytes accessed | tf_op | source)
XLA Modules:
  0.0 118.3 jit_solution(12881748981751932788)
XLA Ops:
  0.6 0.7 iota_compare_fusion.2
  1.3 0.8 copy.7
  2.1 0.7 fusion.1
  2.8 0.1 reduce_window_sum.11
  2.9 0.8 select_reduce_fusion
  3.8 0.2 and_reduce_fusion
  3.9 0.2 fusion
  4.1 0.1 reshape.124
  4.2 0.5 fusion.2.alive_ref
  4.6 0.1 reshape.123.cols_ref
  4.7 0.0 copy-start
  4.8 0.6 gather_fusion
  5.3 0.1 broadcast_select_fusion
  5.4 0.7 select_n.34.rows_ref
  6.0 0.0 copy-done
  6.1 95.6 %shard_map.59 = (f32[12,6,128,256]{3,2,1,0:T(8,128)}, bf16[56,256,128]{2,1,0:T(8,128)(2,1)}, bf16[2,128,1536]{2,1,0:T(8,128)(2,1)}) custom-call(s32[8,12]{1,0:T(8,128)} %copy-done, s32[144]{0:T(256)} %select_n.34.rows_ref, bf16[128,7168]{1,0:T(8,128)(2,1)} %hid_ref.1, bf16[128,2048]{1,0:T(8,128)(2,1)} %grad_ref.1), custom_call_target="tpu_custom_call" | custom-call | tf_op jit(solution)/shard_map/pallas_call | solution.py:307
  101.7 15.0 %shard_map.60 = (f32[144,128,128]{2,1,0:T(8,128)}, f32[12,12,128]{2,1,0:T(8,128)}) custom-call(s32[144]{0:T(256)} %select_n.34.rows_ref, s32[12]{0:T(128)} %fusion.2.alive_ref, f32[12,6,128,256]{3,2,1,0:T(8,128)} %get-tuple-element.7.sums_ref, bf16[56,256,128]{2,1,0:T(8,128)(2,1)} %get-tuple-element.8.h_ref, bf16[256,1536]{1,0:T(8,128)(2,1)} %bitcast.11), custom_call_target="tpu_custom_call" | custom-call | tf_op jit(solution)/shard_map/pallas_call | solution.py:354
  116.6 1.0 reduce_sum.29
  117.6 0.6 sqrt.14
  (5 shorter events, 0.0 us)
Async XLA Ops:
  4.7 1.3 %copy-start = (s32[8,12]{1,0:T(8,128)}, s32[8,12]{1,0:T(8,128)S(1)}, u32[]{:S(2)}) copy-start(s32[8,12]{1,0:T(8,128)S(1)} %reshape.123.cols_ref) | copy-start | bytes 1156

commit v3 on v1

--- a/solution.py
+++ b/solution.py
@@ -10,6 +10,7 @@
 BS = 128
 MESH = pl.DeviceIdType.MESH
 CHUNKS = 4
+HALVES = 2
 
 
 epsilon = 1e-06
@@ -101,23 +102,37 @@
         sent.append(copy)
         return copy
 
-    def part(k):
-        return pl.ds(k * part_rows, part_rows)
+    half_rows = part_rows // HALVES
+
+    def part(k, half):
+        return pl.ds(k * part_rows + half * half_rows, half_rows)
+
+    def held(half):
+        return pl.ds(half * half_rows, half_rows)
 
     def quarter(k):
         return pl.ds(k * part_cols, part_cols)
 
-    own_grad = pltpu.make_async_copy(
-        grad_ref.at[part(t)], gz.at[:, quarter(t)], local_sem.at[0]
-    )
-    stage1 = []
-    for s in range(1, teams):
-        target = (t + s) % teams
-        copy = remote(grad_ref.at[part(target)], gz.at[:, quarter(t)], (b, target, d))
-        copy.start()
-        stage1.append(copy)
-        sent.append(copy)
-    own_grad.start()
+    own_grad, stage1 = [], []
+    for half in range(HALVES):
+        for s in range(1, teams):
+            target = (t + s) % teams
+            copy = remote(
+                grad_ref.at[part(target, half)],
+                gz.at[held(half), quarter(t)],
+                (b, target, d),
+            )
+            copy.start()
+            stage1.append(copy)
+            sent.append(copy)
+        own_grad.append(
+            pltpu.make_async_copy(
+                grad_ref.at[part(t, half)],
+                gz.at[held(half), quarter(t)],
+                local_sem.at[1 + half],
+            )
+        )
+        own_grad[half].start()
 
     order_x = list(range(CHUNKS))
     order_y = order_x[CHUNKS // 2 :] + order_x[: CHUNKS // 2]
@@ -125,30 +140,36 @@
     from_x, from_y, from_sib = {}, {}, []
     from_x[order_x[0]] = send_own(X, order_x[0])
     from_y[order_y[0]] = send_own(Y, order_y[0])
-    own_hidden = pltpu.make_async_copy(hid_ref, hfull.at[mine], local_sem.at[1])
+    own_hidden = pltpu.make_async_copy(hid_ref, hfull.at[mine], local_sem.at[0])
     own_hidden.start()
 
-    own_grad.wait()
-    for copy in stage1:
-        copy.wait_recv()
-
-    for c in range(gcol.shape[0]):
-        gcol[c] = gz[:, c * BS : (c + 1) * BS]
-
-    def pick(p, carry):
-        for j in range(picks):
-            snd[p, :, j * BS : (j + 1) * BS] = gcol[cols_ref[p, j]]
-        return carry
-
-    lax.fori_loop(0, panels, pick, 0)
-    stage2 = []
-    for flip in flips:
-        copy = remote(snd.at[panel_of(*flip)], gfull.at[mine, part(t)], device(*flip))
-        copy.start()
-        stage2.append(copy)
-        sent.append(copy)
-    own_pick = pltpu.make_async_copy(snd.at[mine], gfull.at[mine, part(t)], local_sem.at[2])
-    own_pick.start()
+    own_pick, stage2 = [], []
+    for half in range(HALVES):
+        own_grad[half].wait()
+        for copy in stage1[half * (teams - 1) : (half + 1) * (teams - 1)]:
+            copy.wait_recv()
+        rows = slice(half * half_rows, (half + 1) * half_rows)
+        for c in range(gcol.shape[1]):
+            gcol[half, c] = gz[rows, c * BS : (c + 1) * BS]
+
+        def pick(p, carry):
+            for j in range(picks):
+                snd[half, p, :, j * BS : (j + 1) * BS] = gcol[half, cols_ref[p, j]]
+            return carry
+
+        lax.fori_loop(0, panels, pick, 0)
+        landing = gfull.at[mine, part(t, half)]
+        for flip in flips:
+            copy = remote(snd.at[half, panel_of(*flip)], landing, device(*flip))
+            copy.start()
+            stage2.append(copy)
+            sent.append(copy)
+        own_pick.append(
+            pltpu.make_async_copy(
+                snd.at[half, mine], landing, local_sem.at[1 + HALVES + half]
+            )
+        )
+        own_pick[half].start()
 
     for i in range(1, CHUNKS):
         from_x[order_x[i]] = send_own(X, order_x[i])
@@ -156,39 +177,45 @@
     for c in range(CHUNKS):
         from_sib.append(send_own(SIB, c))
 
-    own_pick.wait()
-    for copy in stage2:
-        copy.wait_recv()
-
     chain_base = counter[0]
-    counter[0] += 2 * (teams - 1)
-
-    def chain(up, k, shard, target):
-        piece = gfull.at[:, part(shard)]
-        slot = chain_base + (k if up else teams - 1 + k)
-        return remote(piece, piece, (b, target, d), slot)
-
-    def chain_send(k, wait):
+    counter[0] += 2 * (teams - 1) * HALVES
+
+    def chain(up, k, shard, target, half):
+        piece = gfull.at[:, part(shard, half)]
+        step = k if up else teams - 1 + k
+        return remote(piece, piece, (b, target, d), chain_base + step * HALVES + half)
+
+    def chain_send(k, half, wait):
         @pl.when((t < teams - 1) & (t - k >= 0))
         def _():
-            copy = chain(True, k, t - k, t + 1)
+            copy = chain(True, k, t - k, t + 1, half)
             copy.wait_send() if wait else copy.start()
 
         @pl.when((t > 0) & (t + k < teams))
         def _():
-            copy = chain(False, k, t + k, t - 1)
+            copy = chain(False, k, t + k, t - 1, half)
             copy.wait_send() if wait else copy.start()
 
-    def chain_recv(k):
+    def chain_recv(k, half):
         @pl.when(t - 1 - k >= 0)
         def _():
-            chain(True, k, t - 1 - k, t - 1).wait_recv()
+            chain(True, k, t - 1 - k, t - 1, half).wait_recv()
 
         @pl.when(t + 1 + k < teams)
         def _():
-            chain(False, k, t + 1 + k, t + 1).wait_recv()
-
-    chain_send(0, False)
+            chain(False, k, t + 1 + k, t + 1, half).wait_recv()
+
+    def chain_step(k):
+        for half in range(HALVES):
+            chain_recv(k, half)
+            if k < teams - 2:
+                chain_send(k + 1, half, False)
+
+    for half in range(HALVES):
+        own_pick[half].wait()
+        for copy in stage2[half * len(flips) : (half + 1) * len(flips)]:
+            copy.wait_recv()
+        chain_send(0, half, False)
 
     panel_x, panel_y, panel_xy = panel_of(*X), panel_of(*Y), panel_of(1, 1, 0)
     from_xy = {}
@@ -204,25 +231,22 @@
             from_xy[cy] = forward(panel_y, X, cy)
         from_sib.append(forward(panel_y, SIB, cy))
         if i % 2 == 1 and steps < teams - 1:
-            chain_recv(steps)
+            chain_step(steps)
             steps += 1
-            if steps < teams - 1:
-                chain_send(steps, False)
     for c in order_x:
         c = order_x[c // 2] if c % 2 == 0 else order_y[c // 2]
         from_xy[c].wait_recv()
         from_sib.append(forward(panel_xy, SIB, c))
     while steps < teams - 1:
-        chain_recv(steps)
+        chain_step(steps)
         steps += 1
-        if steps < teams - 1:
-            chain_send(steps, False)
     for copy in from_sib:
         copy.wait_recv()
     for copy in sent:
         copy.wait_send()
     for k in range(teams - 1):
-        chain_send(k, True)
+        for half in range(HALVES):
+            chain_send(k, half, True)
     own_hidden.wait()
 
 
@@ -230,7 +254,8 @@
     teams = lax.axis_size("team")
     panel_rows, units = hidden.shape
     picks = columns.shape[1]
-    copies = (teams - 1) + 7 + 3 * CHUNKS + 4 * CHUNKS + 2 * (teams - 1)
+    copies = (3 * (teams - 1) + panels - 1) * HALVES + 7 * CHUNKS
+    half_rows = panel_rows // teams // HALVES
     hbm = pl.BlockSpec(memory_space=pl.ANY)
     return pl.pallas_call(
         gather_kernel,
@@ -243,12 +268,12 @@
         scratch_shapes=[
             pltpu.VMEM((panel_rows // teams, teams * out_grad.shape[1]), out_grad.dtype),
             pltpu.VMEM(
-                (teams * out_grad.shape[1] // BS, panel_rows // teams, BS), out_grad.dtype
+                (HALVES, teams * out_grad.shape[1] // BS, half_rows, BS), out_grad.dtype
             ),
-            pltpu.VMEM((panels, panel_rows // teams, picks * BS), out_grad.dtype),
+            pltpu.VMEM((HALVES, panels, half_rows, picks * BS), out_grad.dtype),
             pltpu.SemaphoreType.DMA((copies,)),
             pltpu.SemaphoreType.DMA((copies,)),
-            pltpu.SemaphoreType.DMA((3,)),
+            pltpu.SemaphoreType.DMA((1 + 2 * HALVES,)),
         ],
         compiler_params=pltpu.CompilerParams(collective_id=0, has_side_effects=True),
     )(columns, hidden, out_grad)

time: 117 us -> 109 us (0.932)
  Pallas kernels: 109 us -> 100 us
    pallas_call x1, Pallas kernels: 87.6 us -> 79.1 us  [gather(): pl.pallas_call(gather_kernel, out_shape=(jax.ShapeDtypeStruct((panels, pa...]
where the time goes in v3:
time: 109 us; the launch traced here: 108 us
  Pallas kernels  100 us (92%)
  other arithmetic  4.27 us (4%)
  local copies, waits for them, and re-layouts  2.8 us (3%)
    pallas_call x1, Pallas kernels, gather(): pl.pallas_call(gather_kernel, out_shape=(jax.ShapeDtypeStruct((panels, pa...  79.1 us
    pallas_call x1, Pallas kernels, blocks(): pl.pallas_call(block_kernel, out_shape=(jax.ShapeDtypeStruct((picks * per...  21.3 us

profile of v3, /device:TPU:0, one launch (start us, length us, event | category | flops | bytes accessed | tf_op | source)
XLA Modules:
  0.0 108.2 jit_solution(10581410392722152230)
XLA Ops:
  0.6 0.7 iota_compare_fusion.2
  1.3 0.8 copy.7
  2.1 0.7 fusion.1
  2.8 0.1 reduce_window_sum.11
  2.9 0.8 select_reduce_fusion
  3.8 0.2 and_reduce_fusion
  3.9 0.2 fusion
  4.1 0.1 reshape.127
  4.2 0.5 fusion.2.alive_ref
  4.7 0.1 reshape.126.cols_ref
  4.8 0.0 copy-start
  4.8 0.6 gather_fusion
  5.4 0.1 broadcast_select_fusion
  5.4 0.7 select_n.34.rows_ref
  6.1 0.0 copy-done
  6.1 79.1 %shard_map.59 = (bf16[8,128,7168]{2,1,0:T(8,128)(2,1)}, bf16[8,128,1536]{2,1,0:T(8,128)(2,1)}) custom-call(s32[8,12]{1,0:T(8,128)} %copy-done, bf16[128,7168]{1,0:T(8,128)(2,1)} %hid_ref.1, bf16[128,2048]{1,0:T(8,128)(2,1)} %grad_ref.1), custom_call_target="tpu_custom_call" | custom-call | tf_op jit(solution)/shard_map/pallas_call | solution.py:260
  85.2 21.3 %shard_map.60 = (f32[144,128,128]{2,1,0:T(8,128)}, f32[12,12,128]{2,1,0:T(8,128)}) custom-call(s32[144]{0:T(256)} %select_n.34.rows_ref, s32[12]{0:T(128)} %fusion.2.alive_ref, bf16[1024,7168]{1,0:T(8,128)(2,1)} %bitcast.12, bf16[1024,1536]{1,0:T(8,128)(2,1)} %bitcast.13), custom_call_target="tpu_custom_call" | custom-call | tf_op jit(solution)/shard_map/pallas_call | solution.py:305
  106.5 1.0 reduce_sum.29
  107.5 0.6 sqrt.14
  (5 shorter events, 0.0 us)
Async XLA Ops:
  4.8 1.3 %copy-start = (s32[8,12]{1,0:T(8,128)}, s32[8,12]{1,0:T(8,128)S(1)}, u32[]{:S(2)}) copy-start(s32[8,12]{1,0:T(8,128)S(1)} %reshape.126.cols_ref) | copy-start | bytes 1156

commit v4 on v3

--- a/solution.py
+++ b/solution.py
@@ -283,19 +283,21 @@
     j = pl.program_id(0)
     per_column = out_ref.shape[0]
     scale = alive_ref[j].astype(jnp.float32)
-    g_t = g_ref[...].T
-    for k in range(0, per_column, 2):
-        pair = []
-        for i in (k, k + 1):
+    g = g_ref[...]
+    for k in range(0, per_column, 4):
+        group = []
+        for i in range(k, k + 4):
             r = rows_ref[j * per_column + i]
-            pair.append(h_ref[:, pl.ds(pl.multiple_of(r * BS, BS), BS)])
-        both = jnp.dot(
-            g_t, jnp.concatenate(pair, axis=1), preferred_element_type=jnp.float32
-        )
-        for i in range(2):
-            block = both[:, i * BS : (i + 1) * BS].T * scale
-            out_ref[k + i] = block
-            ssq_ref[0, k + i, :] = jnp.sum(block * block, axis=0)
+            group.append(h_ref[:, pl.ds(pl.multiple_of(r * BS, BS), BS)])
+        product = lax.dot_general(
+            jnp.concatenate(group, axis=1),
+            g,
+            (((0,), (0,)), ((), ())),
+            preferred_element_type=jnp.float32,
+        )
+        block = product.reshape(4, BS, BS) * scale
+        out_ref[k : k + 4] = block
+        ssq_ref[0, k : k + 4, :] = jnp.sum(block * block, axis=1)
 
 
 def blocks(rows, alive, hidden, grad):

time: 109 us -> 108 us (level)
  no operation moved by 1% of the time
where the time goes in v4:
time: 108 us; the launch traced here: 107 us
  Pallas kernels  99.5 us (92%)
  other arithmetic  4.27 us (4%)
  local copies, waits for them, and re-layouts  2.8 us (3%)
    pallas_call x1, Pallas kernels, gather(): pl.pallas_call(gather_kernel, out_shape=(jax.ShapeDtypeStruct((panels, pa...  79.1 us
    pallas_call x1, Pallas kernels, blocks(): pl.pallas_call(block_kernel, out_shape=(jax.ShapeDtypeStruct((picks * per...  20.4 us

profile of v4, /device:TPU:0, one launch (start us, length us, event | category | flops | bytes accessed | tf_op | source)
XLA Modules:
  0.0 107.3 jit_solution(6852364457405215764)
XLA Ops:
  0.6 0.7 iota_compare_fusion.2
  1.3 0.8 copy.7
  2.1 0.7 fusion.1
  2.8 0.1 reduce_window_sum.11
  2.9 0.8 select_reduce_fusion
  3.8 0.2 and_reduce_fusion
  3.9 0.2 fusion
  4.1 0.1 reshape.127
  4.2 0.5 fusion.2.alive_ref
  4.7 0.1 reshape.126.cols_ref
  4.8 0.0 copy-start
  4.8 0.6 gather_fusion
  5.4 0.1 broadcast_select_fusion
  5.4 0.7 select_n.34.rows_ref
  6.1 0.0 copy-done
  6.1 79.1 %shard_map.59 = (bf16[8,128,7168]{2,1,0:T(8,128)(2,1)}, bf16[8,128,1536]{2,1,0:T(8,128)(2,1)}) custom-call(s32[8,12]{1,0:T(8,128)} %copy-done, bf16[128,7168]{1,0:T(8,128)(2,1)} %hid_ref.1, bf16[128,2048]{1,0:T(8,128)(2,1)} %grad_ref.1), custom_call_target="tpu_custom_call" | custom-call | tf_op jit(solution)/shard_map/pallas_call | solution.py:260
  85.2 20.4 %shard_map.60 = (f32[144,128,128]{2,1,0:T(8,128)}, f32[12,12,128]{2,1,0:T(8,128)}) custom-call(s32[144]{0:T(256)} %select_n.34.rows_ref, s32[12]{0:T(128)} %fusion.2.alive_ref, bf16[1024,7168]{1,0:T(8,128)(2,1)} %bitcast.12, bf16[1024,1536]{1,0:T(8,128)(2,1)} %bitcast.13), custom_call_target="tpu_custom_call" | custom-call | tf_op jit(solution)/shard_map/pallas_call | solution.py:307
  105.6 1.0 reduce_sum.29
  106.6 0.6 sqrt.14
  (5 shorter events, 0.0 us)
Async XLA Ops:
  4.8 1.3 %copy-start = (s32[8,12]{1,0:T(8,128)}, s32[8,12]{1,0:T(8,128)S(1)}, u32[]{:S(2)}) copy-start(s32[8,12]{1,0:T(8,128)S(1)} %reshape.126.cols_ref) | copy-start | bytes 1156
